TPU v7x, 256 devices: a whole 4x4x8 slice. The times are simulated.
256 devices in a mesh: cuts: 8 (over x_lo, y), gz: 32 (over z, x_hi, core).
Axes of the slice: x: 4 (x_hi: 2, x_lo: 2; x = x_hi * 2 + x_lo), y: 4, z: 8, core: 2. Of those that a mesh axis runs over, the one named last changes fastest.
Arguments:
- vectors: float32 [8, 32, 64, 128, 128], P('cuts', None, 'gz'), may hold values from -9 to 9
- onsite: float32 [64, 128, 128], P('gz'), may hold values from -8.25 to 8.25
- center: float32 [8], P('cuts'), may hold values from -3 to 3
- inv_half: float32 [8], P('cuts'), may hold values from 0.06 to 0.1
- cheb_coef: float32 [8, 3], P('cuts'), may hold values from 0.5 to 1.5
Outputs:
- basis: float32 [8, 64, 64, 128, 128], P('cuts', None, 'gz')
- projected: float32 [8, 64, 64], P('cuts')
All inputs are finite; a program needn't handle non-finite values.
Results may differ from a plain program's by a relative error of at most 0.00018.
Values sent between devices are 32-bit elements; how exact they have to be, the bound alone decides.
A program may use at most 128 MiB of HBM per device.

v0:
```python
import jax
import jax.numpy as jnp
from jax import lax
from jax.sharding import PartitionSpec as P


def padded_2(array, sides, width):
    for axis, dim in sides:
        size, length = (lax.axis_size(axis), array.shape[dim])
        up = [(i, (i + 1) % size) for i in range(size)]
        down = [(j, i) for i, j in up]
        last = lax.slice_in_dim(array, length - width, length, axis=dim)
        leading = lax.slice_in_dim(array, 0, width, axis=dim)
        before = lax.ppermute(last, axis, up)
        after = lax.ppermute(leading, axis, down)
        array = jnp.concatenate([before, array, after], axis=dim)
    return array


def from_behind(block, axis, distance):
    devices = range(lax.axis_size(axis))
    route = [(i - distance, i) for i in devices if i - distance in devices]
    return lax.ppermute(block, axis, route)


def neighbours_xy(middle):
    padded = jnp.pad(middle, ((0, 0), (0, 0), (1, 1), (1, 1)))
    return (
        padded[:, :, 2:, 1:-1]
        + padded[:, :, :-2, 1:-1]
        + padded[:, :, 1:-1, 2:]
        + padded[:, :, 1:-1, :-2]
    )


def hamiltonian(extended, onsite_part):
    middle = extended[:, 1:-1]
    along_z = extended[:, 2:] + extended[:, :-2]
    return onsite_part[None] * middle - along_z - neighbours_xy(middle)


def product(left, right):
    return jnp.dot(left, right, precision=lax.Precision.HIGHEST, preferred_element_type=jnp.float32)


def body(vectors, onsite, center, inv_half, cheb_coef):
    field = vectors[0]
    count = field.shape[0]
    layers = field.shape[1]
    sites_all = layers * lax.axis_size("gz") * field.shape[2] * field.shape[3]
    identity = jnp.eye(2 * count, dtype=jnp.float32)

    def scaled(extended, onsite_part):
        return inv_half[0] * (hamiltonian(extended, onsite_part) - center[0] * extended[:, 1:-1])

    def filter_step(values):
        return padded_2(values, (("gz", 1),), 1)

    first = scaled(filter_step(field), onsite)
    second = 2.0 * scaled(filter_step(first), onsite) - field
    filtered = cheb_coef[0, 0] * field + cheb_coef[0, 1] * first + cheb_coef[0, 2] * second
    partner = from_behind(filtered, "cuts", -1)
    union = jnp.concatenate([filtered, partner], 0).reshape(2 * count, -1)
    gram = lax.psum(product(union, union.T), "gz") / sites_all + 0.25 * identity
    factor = jnp.linalg.cholesky(gram)
    inverse = jax.scipy.linalg.solve_triangular(factor, identity, lower=True)
    basis = product(inverse, union)
    shaped = basis.reshape(2 * count, layers, field.shape[2], field.shape[3])
    images = hamiltonian(padded_2(shaped, (("gz", 1),), 1), onsite).reshape(2 * count, -1)
    projected = lax.psum(product(basis, images.T), "gz") / sites_all
    return (basis.reshape(1, 2 * count, layers, field.shape[2], field.shape[3]), projected[None])


def solution(mesh):
    in_specs = (
        P("cuts", None, "gz", None, None),
        P("gz", None, None),
        P("cuts"),
        P("cuts"),
        P("cuts", None),
    )
    out_specs = (P("cuts", None, "gz", None, None), P("cuts", None, None))
    return jax.shard_map(body, mesh=mesh, in_specs=in_specs, out_specs=out_specs, check_vma=False)
```

profile of v0, /device:TPU:24, one launch (start us, length us, event | category | flops | bytes accessed | tf_op | source)
XLA Modules:
  0.0 651.8 jit_solution(12368654120373299613)
XLA Ops:
  0.6 4.6 copy.28
  5.7 7.8 %collective-permute-start = (f32[32,1,128,128]{3,0,2,1:T(8,128)S(1)}, f32[32,1,128,128]{3,0,2,1:T(8,128)S(1)}, u32[]{:S(2)}, u32[]{:S(2)}) collective-permute-start(f32[32,1,128,128]{3,0,2,1:T(8,128)S(1)} %get-tuple-element.6), channel_id=1, source_target_pairs={{1,0},{2,1},{3,2},{4,3},{5,4},{6,5},{7,6},{8,7},{9,8},{10,9},{11,1... | collective-permute-start | bytes 6291464 | tf_op jit(solution)/shard_map/ppermute | solution.py:15
  14.8 22.3 %collective-permute-done = f32[32,1,128,128]{3,0,2,1:T(8,128)S(1)} collective-permute-done((f32[32,1,128,128]{3,0,2,1:T(8,128)S(1)}, f32[32,1,128,128]{3,0,2,1:T(8,128)S(1)}, u32[]{:S(2)}, u32[]{:S(2)}) %collective-permute-start) | collective-permute-done | bytes 2097184 | tf_op jit(solution)/shard_map/ppermute | solution.py:15
  37.1 5.6 collective-permute-done.1
  42.7 3.5 fusion.17
  46.8 34.3 %collective-permute-start.3 = (f32[32,1,128,128]{3,0,2,1:T(8,128)S(1)}, f32[32,1,128,128]{3,0,2,1:T(8,128)S(1)}, u32[]{:S(2)}, u32[]{:S(2)}) collective-permute-start(f32[32,1,128,128]{3,0,2,1:T(8,128)S(1)} %get-tuple-element.5), channel_id=1, source_target_pairs={{0,1},{1,2},{2,3},{3,4},{4,5},{5,6},{6,7},{7,8},{8,9},{9,10},{10,1... | collective-permute-start | bytes 6291464 | tf_op jit(solution)/shard_map/ppermute | solution.py:14
  81.7 2.9 collective-permute-done.2
  84.6 29.4 %collective-permute-done.3 = f32[32,1,128,128]{3,0,2,1:T(8,128)S(1)} collective-permute-done((f32[32,1,128,128]{3,0,2,1:T(8,128)S(1)}, f32[32,1,128,128]{3,0,2,1:T(8,128)S(1)}, u32[]{:S(2)}, u32[]{:S(2)}) %collective-permute-start.3) | collective-permute-done | bytes 2097184 | tf_op jit(solution)/shard_map/ppermute | solution.py:14
  115.4 9.1 %fusion.27 = f32[32,2,128,128]{3,0,2,1:T(8,128)S(1)} fusion(f32[32,2,128,128]{3,0,2,1:T(8,128)S(1)} %fusion.17, f32[32,1,128,128]{3,0,2,1:T(8,128)} %copy-done.4, f32[32,1,128,128]{3,0,2,1:T(8,128)S(1)} %collective-permute-done.2, f32[]{:T(128)} %bitcast.5, f32[]{:T(128)} %bitcast.44, f32[2,128,128]{2,1,0:T(8,128)S(1)} %copy-done.5, f32[]{:T(128)} %bitcast.46, ...), kind=kLoop, calls=%fused_computation.42 | loop fusion | flops 19922944 | bytes 16908308 | tf_op jit(solution)/shard_map/add | solution.py:61
  124.5 2.9 collective-permute-start.4
  127.5 74.5 %collective-permute-done.4 = f32[32,2,128,128]{3,0,2,1:T(8,128)S(1)} collective-permute-done((f32[32,2,128,128]{3,0,2,1:T(8,128)S(1)}, f32[32,2,128,128]{3,0,2,1:T(8,128)S(1)}, u32[]{:S(2)}, u32[]{:S(2)}) %collective-permute-start.4) | collective-permute-done | bytes 4194336 | tf_op jit(solution)/shard_map/ppermute | solution.py:23
  204.0 6.6 %convolution_bitcast_fusion = f32[64,64]{1,0:T(8,128)S(1)} fusion(f32[32,2,128,128]{3,0,2,1:T(8,128)S(1)} %collective-permute-done.4, f32[32,2,128,128]{3,0,2,1:T(8,128)S(1)} %fusion.27), kind=kOutput, calls=%fused_computation.52 | convolution fusion | flops 1612709888 | bytes 8404992 | tf_op jit(solution)/shard_map/dot_general | solution.py:43
  210.6 149.8 %psum.14 = f32[64,64]{1,0:T(8,128)S(1)} all-reduce(f32[64,64]{1,0:T(8,128)S(1)} %convolution_bitcast_fusion), channel_id=1, replica_groups=mesh['cuts'=8,'gz'=32] {'gz'}, use_global_device_ids=true, to_apply=%region_0.1 | all-reduce | flops 4096 | bytes 32768 | tf_op jit(solution)/shard_map/psum | solution.py:64
  360.5 4.5 pad_maximum_fusion.2
  365.0 8.3 %copy.11 = f32[64,2,128,128]{3,2,1,0:T(8,128)} copy(f32[64,2,128,128]{3,0,2,1:T(8,128)S(1)} %pad_maximum_fusion.2) | data formatting | bytes 16777216 | tf_op jit(solution)/shard_map/concatenate | solution.py:63
  373.4 5.8 cholesky.17
  380.6 4.9 custom-call.7
  385.7 16.2 %fusion.7 = f32[64,32768]{1,0:T(8,128)S(1)} fusion(f32[64,64]{1,0:T(8,128)S(1)} %fusion.33, f32[8,8,256,128]{3,2,1,0:T(8,128)} %bitcast.54), kind=kOutput, calls=%fused_computation.19 | convolution fusion | flops 1610612736 | bytes 16793600 | tf_op jit(solution)/shard_map/dot_general | solution.py:43
  403.4 4.2 fusion.36
  408.1 45.9 %collective-permute-done.5 = f32[64,1,128,128]{3,2,1,0:T(8,128)} collective-permute-done((f32[64,1,128,128]{3,2,1,0:T(8,128)}, f32[64,1,128,128]{3,2,1,0:T(8,128)}, u32[]{:S(2)}, u32[]{:S(2)}) %collective-permute-start.5) | collective-permute-done | bytes 4194336 | tf_op jit(solution)/shard_map/ppermute | solution.py:15
  454.0 5.6 collective-permute-done.6
  459.6 10.0 %fusion.3 = f32[64,2,128,128]{3,2,1,0:T(8,128)} fusion(f32[64,2,128,128]{3,2,1,0:T(8,128)S(1)} %bitcast.48, f32[64,1,128,128]{3,2,1,0:T(8,128)} %collective-permute-done.6, f32[64,1,128,128]{3,2,1,0:T(8,128)} %collective-permute-done.5, f32[2,128,128]{2,1,0:T(8,128)S(1)} %copy-done.5), kind=kLoop, calls=%fused_computation.15 | loop fusion | flops 18874368 | bytes 25296896 | tf_op jit(solution)/shard_map/sub | solution.py:39
  469.5 15.6 %fusion.4 = f32[64,64]{1,0:T(8,128)S(1)} fusion(f32[64,32768]{1,0:T(8,128)S(1)} %fusion.7, f32[8,8,256,128]{3,2,1,0:T(8,128)} %bitcast.53), kind=kOutput, calls=%fused_computation.16 | convolution fusion | flops 1610612736 | bytes 16793600 | tf_op jit(solution)/shard_map/dot_general | solution.py:43
  485.2 165.7 %psum.15 = f32[64,64]{1,0:T(8,128)S(1)} all-reduce(f32[64,64]{1,0:T(8,128)S(1)} %fusion.4), channel_id=1, replica_groups=mesh['cuts'=8,'gz'=32] {'gz'}, use_global_device_ids=true, to_apply=%region_3.4 | all-reduce | flops 4096 | bytes 32768 | tf_op jit(solution)/shard_map/psum | solution.py:70
  (30 shorter events, 9.3 us)
Async XLA Ops:
  5.2 37.5 %copy-start.5 = (f32[2,128,128]{2,1,0:T(8,128)S(1)}, f32[2,128,128]{2,1,0:T(8,128)}, u32[]{:S(2)}) copy-start(f32[2,128,128]{2,1,0:T(8,128)} %param.6) | copy-start | bytes 393220
  5.7 31.4 %collective-permute-start = (f32[32,1,128,128]{3,0,2,1:T(8,128)S(1)}, f32[32,1,128,128]{3,0,2,1:T(8,128)S(1)}, u32[]{:S(2)}, u32[]{:S(2)}) collective-permute-start(f32[32,1,128,128]{3,0,2,1:T(8,128)S(1)} %get-tuple-element.6), channel_id=1, source_target_pairs={{1,0},{2,1},{3,2},{4,3},{5,4},{6,5},{7,6},{8,7},{9,8},{10,9},{11,1... | collective-permute-start | bytes 6291464 | tf_op jit(solution)/shard_map/ppermute | solution.py:15
  13.5 29.2 %collective-permute-start.1 = (f32[32,1,128,128]{3,0,2,1:T(8,128)S(1)}, f32[32,1,128,128]{3,0,2,1:T(8,128)S(1)}, u32[]{:S(2)}, u32[]{:S(2)}) collective-permute-start(f32[32,1,128,128]{3,0,2,1:T(8,128)S(1)} %get-tuple-element.7), channel_id=1, source_target_pairs={{0,1},{1,2},{2,3},{3,4},{4,5},{5,6},{6,7},{7,8},{8,9},{9,10},{10,1... | collective-permute-start | bytes 6291464 | tf_op jit(solution)/shard_map/ppermute | solution.py:14
  46.2 34.9 %copy-start.6 = (f32[1,3]{1,0:T(1,128)S(1)}, f32[1,3]{1,0:T(1,128)}, u32[]{:S(2)}) copy-start(f32[1,3]{1,0:T(1,128)} %param.9) | copy-start | bytes 40
  46.2 69.2 %copy-start.2 = (f32[1,32,2,128,128]{4,3,2,1,0:T(8,128)S(1)}, f32[1,32,2,128,128]{4,3,2,1,0:T(8,128)}, u32[]{:S(2)}) copy-start(f32[1,32,2,128,128]{4,3,2,1,0:T(8,128)} %param.5) | copy-start | bytes 12582916
  46.7 38.0 %collective-permute-start.2 = (f32[32,1,128,128]{3,0,2,1:T(8,128)S(1)}, f32[32,1,128,128]{3,0,2,1:T(8,128)S(1)}, u32[]{:S(2)}, u32[]{:S(2)}) collective-permute-start(f32[32,1,128,128]{3,0,2,1:T(8,128)S(1)} %get-tuple-element.4), channel_id=1, source_target_pairs={{1,0},{2,1},{3,2},{4,3},{5,4},{6,5},{7,6},{8,7},{9,8},{10,9},{11,1... | collective-permute-start | bytes 6291464 | tf_op jit(solution)/shard_map/ppermute | solution.py:15
  46.8 67.3 %collective-permute-start.3 = (f32[32,1,128,128]{3,0,2,1:T(8,128)S(1)}, f32[32,1,128,128]{3,0,2,1:T(8,128)S(1)}, u32[]{:S(2)}, u32[]{:S(2)}) collective-permute-start(f32[32,1,128,128]{3,0,2,1:T(8,128)S(1)} %get-tuple-element.5), channel_id=1, source_target_pairs={{0,1},{1,2},{2,3},{3,4},{4,5},{5,6},{6,7},{7,8},{8,9},{9,10},{10,1... | collective-permute-start | bytes 6291464 | tf_op jit(solution)/shard_map/ppermute | solution.py:14
  114.0 1.3 copy-start.4
  124.5 77.5 %copy-start.1 = (f32[32,2,128,128]{3,0,2,1:T(8,128)}, f32[32,2,128,128]{3,0,2,1:T(8,128)S(1)}, u32[]{:S(2)}) copy-start(f32[32,2,128,128]{3,0,2,1:T(8,128)S(1)} %fusion.27) | copy-start | bytes 12582916
  124.5 77.5 %collective-permute-start.4 = (f32[32,2,128,128]{3,0,2,1:T(8,128)S(1)}, f32[32,2,128,128]{3,0,2,1:T(8,128)S(1)}, u32[]{:S(2)}, u32[]{:S(2)}) collective-permute-start(f32[32,2,128,128]{3,0,2,1:T(8,128)S(1)} %fusion.27), channel_id=1, source_target_pairs={{32,0},{64,32},{96,64},{128,96},{160,128},{192,160},{224,192},{33,... | collective-permute-start | bytes 12582920 | tf_op jit(solution)/shard_map/ppermute | solution.py:23
  202.0 2.0 copy-start.3
  403.4 56.1 %copy-start = (f32[8,8,256,128]{3,2,1,0:T(8,128)}, f32[8,8,256,128]{3,2,1,0:T(8,128)S(1)}, u32[]{:S(2)}) copy-start(f32[8,8,256,128]{3,2,1,0:T(8,128)S(1)} %copy.14) | copy-start | bytes 25165828
  407.6 46.4 %collective-permute-start.5 = (f32[64,1,128,128]{3,2,1,0:T(8,128)}, f32[64,1,128,128]{3,2,1,0:T(8,128)}, u32[]{:S(2)}, u32[]{:S(2)}) collective-permute-start(f32[64,1,128,128]{3,2,1,0:T(8,128)} %get-tuple-element.2), channel_id=1, source_target_pairs={{1,0},{2,1},{3,2},{4,3},{5,4},{6,5},{7,6},{8,7},{9,8},{10,9},{11,1... | collective-permute-start | bytes 12582920 | tf_op jit(solution)/shard_map/ppermute | solution.py:15
  407.6 52.0 %collective-permute-start.6 = (f32[64,1,128,128]{3,2,1,0:T(8,128)}, f32[64,1,128,128]{3,2,1,0:T(8,128)}, u32[]{:S(2)}, u32[]{:S(2)}) collective-permute-start(f32[64,1,128,128]{3,2,1,0:T(8,128)} %get-tuple-element.3), channel_id=1, source_target_pairs={{0,1},{1,2},{2,3},{3,4},{4,5},{5,6},{6,7},{7,8},{8,9},{9,10},{10,1... | collective-permute-start | bytes 12582920 | tf_op jit(solution)/shard_map/ppermute | solution.py:14
where the time goes:
time: 659 us; the launch traced here: 652 us
  blocking collectives  316 us (48%)
  waiting for transfers between devices  186 us (28%)
  starting transfers between devices  45.7 us (7%)
  other arithmetic  39.8 us (6%)
  matrix products  38.7 us (6%)
  local copies, waits for them, and re-layouts  23.5 us (4%)
    psum x1, blocking collectives, body(): projected = lax.psum(product(basis, images.T), 'gz') / sites_all  166 us
    psum x1, blocking collectives, body(): gram = lax.psum(product(union, union.T), 'gz') / sites_all + 0.25 * identity  150 us
    ppermute x1, waiting for transfers between devices, from_behind(): return lax.ppermute(block, axis, route)  74.5 us
    ppermute x3, waiting for transfers between devices, padded_2(): after = lax.ppermute(leading, axis, down)  71.1 us
    ppermute x3, waiting for transfers between devices, padded_2(): before = lax.ppermute(last, axis, up)  40.6 us
    dot_general x3, matrix products, product(): jnp.dot(left, right, precision=lax.Precision.HIGHEST, preferred_element_t...  38.5 us
    ppermute x3, starting transfers between devices, padded_2(): before = lax.ppermute(last, axis, up)  34.8 us
  transfers between devices with their start and end apart: 7, of which 7 were waited for; matrix products, arithmetic and copies ran while one was open for 0% of the time, Pallas kernels for 0%

commit v1 on v0

--- a/solution.py
+++ b/solution.py
@@ -2,6 +2,11 @@
 import jax.numpy as jnp
 from jax import lax
 from jax.sharding import PartitionSpec as P
+
+
+def move_ticks_over_axis(w_in):
+    current_arr = jax.lax.all_gather(w_in, "gz")
+    return jnp.sum(current_arr, 0)
 
 
 def padded_2(array, sides, width):
@@ -67,7 +72,7 @@
     basis = product(inverse, union)
     shaped = basis.reshape(2 * count, layers, field.shape[2], field.shape[3])
     images = hamiltonian(padded_2(shaped, (("gz", 1),), 1), onsite).reshape(2 * count, -1)
-    projected = lax.psum(product(basis, images.T), "gz") / sites_all
+    projected = move_ticks_over_axis(product(basis, images.T)) / sites_all
     return (basis.reshape(1, 2 * count, layers, field.shape[2], field.shape[3]), projected[None])
 
 

time: 659 us -> 574 us (0.87)
  blocking collectives: 316 us -> 230 us
    psum x1 -> x0, blocking collectives: 166 us -> none  [body(): projected = lax.psum(product(basis, images.T), 'gz') / sites_all]
    all_gather x0 -> x1, blocking collectives: none -> 80 us  [move_ticks_over_axis(): current_arr = jax.lax.all_gather(w_in, 'gz')]
where the time goes in v1:
time: 574 us; the launch traced here: 566 us
  blocking collectives  230 us (40%)
  waiting for transfers between devices  186 us (32%)
  starting transfers between devices  45.7 us (8%)
  other arithmetic  39.9 us (7%)
  matrix products  38.7 us (7%)
  local copies, waits for them, and re-layouts  23.5 us (4%)
    psum x1, blocking collectives, body(): gram = lax.psum(product(union, union.T), 'gz') / sites_all + 0.25 * identity  150 us
    all_gather x1, blocking collectives, move_ticks_over_axis(): current_arr = jax.lax.all_gather(w_in, 'gz')  80 us
    ppermute x1, waiting for transfers between devices, from_behind(): return lax.ppermute(block, axis, route)  74.5 us
    ppermute x3, waiting for transfers between devices, padded_2(): after = lax.ppermute(leading, axis, down)  71.1 us
    ppermute x3, waiting for transfers between devices, padded_2(): before = lax.ppermute(last, axis, up)  40.6 us
    dot_general x3, matrix products, product(): jnp.dot(left, right, precision=lax.Precision.HIGHEST, preferred_element_t...  38.5 us
    ppermute x3, starting transfers between devices, padded_2(): before = lax.ppermute(last, axis, up)  34.8 us
  transfers between devices with their start and end apart: 7, of which 7 were waited for; matrix products, arithmetic and copies ran while one was open for 0% of the time, Pallas kernels for 0%

profile of v1, /device:TPU:24, one launch (start us, length us, event | category | flops | bytes accessed | tf_op | source)
XLA Modules:
  0.0 566.1 jit_solution(8033019109574350952)
XLA Ops:
  0.6 4.6 copy.28
  5.7 7.8 %collective-permute-start = (f32[32,1,128,128]{3,0,2,1:T(8,128)S(1)}, f32[32,1,128,128]{3,0,2,1:T(8,128)S(1)}, u32[]{:S(2)}, u32[]{:S(2)}) collective-permute-start(f32[32,1,128,128]{3,0,2,1:T(8,128)S(1)} %get-tuple-element.6), channel_id=1, source_target_pairs={{1,0},{2,1},{3,2},{4,3},{5,4},{6,5},{7,6},{8,7},{9,8},{10,9},{11,1... | collective-permute-start | bytes 6291464 | tf_op jit(solution)/shard_map/ppermute | solution.py:20
  14.8 22.3 %collective-permute-done = f32[32,1,128,128]{3,0,2,1:T(8,128)S(1)} collective-permute-done((f32[32,1,128,128]{3,0,2,1:T(8,128)S(1)}, f32[32,1,128,128]{3,0,2,1:T(8,128)S(1)}, u32[]{:S(2)}, u32[]{:S(2)}) %collective-permute-start) | collective-permute-done | bytes 2097184 | tf_op jit(solution)/shard_map/ppermute | solution.py:20
  37.1 5.6 collective-permute-done.1
  42.7 3.5 fusion.17
  46.8 34.3 %collective-permute-start.3 = (f32[32,1,128,128]{3,0,2,1:T(8,128)S(1)}, f32[32,1,128,128]{3,0,2,1:T(8,128)S(1)}, u32[]{:S(2)}, u32[]{:S(2)}) collective-permute-start(f32[32,1,128,128]{3,0,2,1:T(8,128)S(1)} %get-tuple-element.5), channel_id=1, source_target_pairs={{0,1},{1,2},{2,3},{3,4},{4,5},{5,6},{6,7},{7,8},{8,9},{9,10},{10,1... | collective-permute-start | bytes 6291464 | tf_op jit(solution)/shard_map/ppermute | solution.py:19
  81.7 2.9 collective-permute-done.2
  84.6 29.4 %collective-permute-done.3 = f32[32,1,128,128]{3,0,2,1:T(8,128)S(1)} collective-permute-done((f32[32,1,128,128]{3,0,2,1:T(8,128)S(1)}, f32[32,1,128,128]{3,0,2,1:T(8,128)S(1)}, u32[]{:S(2)}, u32[]{:S(2)}) %collective-permute-start.3) | collective-permute-done | bytes 2097184 | tf_op jit(solution)/shard_map/ppermute | solution.py:19
  115.4 9.1 %fusion.27 = f32[32,2,128,128]{3,0,2,1:T(8,128)S(1)} fusion(f32[32,2,128,128]{3,0,2,1:T(8,128)S(1)} %fusion.17, f32[32,1,128,128]{3,0,2,1:T(8,128)} %copy-done.4, f32[32,1,128,128]{3,0,2,1:T(8,128)S(1)} %collective-permute-done.2, f32[]{:T(128)} %bitcast.5, f32[]{:T(128)} %bitcast.45, f32[2,128,128]{2,1,0:T(8,128)S(1)} %copy-done.5, f32[]{:T(128)} %bitcast.47, ...), kind=kLoop, calls=%fused_computation.42 | loop fusion | flops 19922944 | bytes 16908308 | tf_op jit(solution)/shard_map/add | solution.py:66
  124.5 2.9 collective-permute-start.4
  127.5 74.5 %collective-permute-done.4 = f32[32,2,128,128]{3,0,2,1:T(8,128)S(1)} collective-permute-done((f32[32,2,128,128]{3,0,2,1:T(8,128)S(1)}, f32[32,2,128,128]{3,0,2,1:T(8,128)S(1)}, u32[]{:S(2)}, u32[]{:S(2)}) %collective-permute-start.4) | collective-permute-done | bytes 4194336 | tf_op jit(solution)/shard_map/ppermute | solution.py:28
  204.0 6.6 %convolution_bitcast_fusion = f32[64,64]{1,0:T(8,128)S(1)} fusion(f32[32,2,128,128]{3,0,2,1:T(8,128)S(1)} %collective-permute-done.4, f32[32,2,128,128]{3,0,2,1:T(8,128)S(1)} %fusion.27), kind=kOutput, calls=%fused_computation.52 | convolution fusion | flops 1612709888 | bytes 8404992 | tf_op jit(solution)/shard_map/dot_general | solution.py:48
  210.6 149.8 %psum.7 = f32[64,64]{1,0:T(8,128)S(1)} all-reduce(f32[64,64]{1,0:T(8,128)S(1)} %convolution_bitcast_fusion), channel_id=1, replica_groups=mesh['cuts'=8,'gz'=32] {'gz'}, use_global_device_ids=true, to_apply=%region_0.1 | all-reduce | flops 4096 | bytes 32768 | tf_op jit(solution)/shard_map/psum | solution.py:69
  360.5 4.5 pad_maximum_fusion.2
  365.0 8.3 %copy.11 = f32[64,2,128,128]{3,2,1,0:T(8,128)} copy(f32[64,2,128,128]{3,0,2,1:T(8,128)S(1)} %pad_maximum_fusion.2) | data formatting | bytes 16777216 | tf_op jit(solution)/shard_map/concatenate | solution.py:68
  373.4 5.8 %cholesky.17 = f32[64,64]{1,0:T(8,128)S(1)} custom-call(f32[64,64]{1,0:T(8,128)S(1)} %fusion.35), custom_call_target="Cholesky" | custom-call | tf_op jit(solution)/shard_map/jit(cholesky)/cholesky | solution.py:70
  380.6 4.9 custom-call.7
  385.7 16.2 %fusion.7 = f32[64,32768]{1,0:T(8,128)S(1)} fusion(f32[64,64]{1,0:T(8,128)S(1)} %fusion.33, f32[8,8,256,128]{3,2,1,0:T(8,128)} %bitcast.55), kind=kOutput, calls=%fused_computation.19 | convolution fusion | flops 1610612736 | bytes 16793600 | tf_op jit(solution)/shard_map/dot_general | solution.py:48
  403.4 4.2 fusion.36
  408.1 45.9 %collective-permute-done.5 = f32[64,1,128,128]{3,2,1,0:T(8,128)} collective-permute-done((f32[64,1,128,128]{3,2,1,0:T(8,128)}, f32[64,1,128,128]{3,2,1,0:T(8,128)}, u32[]{:S(2)}, u32[]{:S(2)}) %collective-permute-start.5) | collective-permute-done | bytes 4194336 | tf_op jit(solution)/shard_map/ppermute | solution.py:20
  454.0 5.6 collective-permute-done.6
  459.6 10.0 %fusion.3 = f32[64,2,128,128]{3,2,1,0:T(8,128)} fusion(f32[64,2,128,128]{3,2,1,0:T(8,128)S(1)} %bitcast.49, f32[64,1,128,128]{3,2,1,0:T(8,128)} %collective-permute-done.6, f32[64,1,128,128]{3,2,1,0:T(8,128)} %collective-permute-done.5, f32[2,128,128]{2,1,0:T(8,128)S(1)} %copy-done.5), kind=kLoop, calls=%fused_computation.15 | loop fusion | flops 18874368 | bytes 25296896 | tf_op jit(solution)/shard_map/sub | solution.py:44
  469.5 15.6 %fusion.4 = f32[64,64]{1,0:T(8,128)S(1)} fusion(f32[64,32768]{1,0:T(8,128)S(1)} %fusion.7, f32[8,8,256,128]{3,2,1,0:T(8,128)} %bitcast.54), kind=kOutput, calls=%fused_computation.16 | convolution fusion | flops 1610612736 | bytes 16793600 | tf_op jit(solution)/shard_map/dot_general | solution.py:48
  485.2 80.0 %all-gather = f32[2048,64]{1,0:T(8,128)S(1)} all-gather(f32[64,64]{1,0:T(8,128)S(1)} %fusion.4), channel_id=2, replica_groups=mesh['cuts'=8,'gz'=32] {'gz'}, dimensions={0}, use_global_device_ids=true | all-gather | bytes 540672 | tf_op jit(solution)/shard_map/all_gather | solution.py:8
  (31 shorter events, 9.3 us)
Async XLA Ops:
  5.2 37.5 %copy-start.5 = (f32[2,128,128]{2,1,0:T(8,128)S(1)}, f32[2,128,128]{2,1,0:T(8,128)}, u32[]{:S(2)}) copy-start(f32[2,128,128]{2,1,0:T(8,128)} %param.6) | copy-start | bytes 393220
  5.7 31.4 %collective-permute-start = (f32[32,1,128,128]{3,0,2,1:T(8,128)S(1)}, f32[32,1,128,128]{3,0,2,1:T(8,128)S(1)}, u32[]{:S(2)}, u32[]{:S(2)}) collective-permute-start(f32[32,1,128,128]{3,0,2,1:T(8,128)S(1)} %get-tuple-element.6), channel_id=1, source_target_pairs={{1,0},{2,1},{3,2},{4,3},{5,4},{6,5},{7,6},{8,7},{9,8},{10,9},{11,1... | collective-permute-start | bytes 6291464 | tf_op jit(solution)/shard_map/ppermute | solution.py:20
  13.5 29.2 %collective-permute-start.1 = (f32[32,1,128,128]{3,0,2,1:T(8,128)S(1)}, f32[32,1,128,128]{3,0,2,1:T(8,128)S(1)}, u32[]{:S(2)}, u32[]{:S(2)}) collective-permute-start(f32[32,1,128,128]{3,0,2,1:T(8,128)S(1)} %get-tuple-element.7), channel_id=1, source_target_pairs={{0,1},{1,2},{2,3},{3,4},{4,5},{5,6},{6,7},{7,8},{8,9},{9,10},{10,1... | collective-permute-start | bytes 6291464 | tf_op jit(solution)/shard_map/ppermute | solution.py:19
  46.2 34.9 %copy-start.6 = (f32[1,3]{1,0:T(1,128)S(1)}, f32[1,3]{1,0:T(1,128)}, u32[]{:S(2)}) copy-start(f32[1,3]{1,0:T(1,128)} %param.9) | copy-start | bytes 40
  46.2 69.2 %copy-start.2 = (f32[1,32,2,128,128]{4,3,2,1,0:T(8,128)S(1)}, f32[1,32,2,128,128]{4,3,2,1,0:T(8,128)}, u32[]{:S(2)}) copy-start(f32[1,32,2,128,128]{4,3,2,1,0:T(8,128)} %param.5) | copy-start | bytes 12582916
  46.7 38.0 %collective-permute-start.2 = (f32[32,1,128,128]{3,0,2,1:T(8,128)S(1)}, f32[32,1,128,128]{3,0,2,1:T(8,128)S(1)}, u32[]{:S(2)}, u32[]{:S(2)}) collective-permute-start(f32[32,1,128,128]{3,0,2,1:T(8,128)S(1)} %get-tuple-element.4), channel_id=1, source_target_pairs={{1,0},{2,1},{3,2},{4,3},{5,4},{6,5},{7,6},{8,7},{9,8},{10,9},{11,1... | collective-permute-start | bytes 6291464 | tf_op jit(solution)/shard_map/ppermute | solution.py:20
  46.8 67.3 %collective-permute-start.3 = (f32[32,1,128,128]{3,0,2,1:T(8,128)S(1)}, f32[32,1,128,128]{3,0,2,1:T(8,128)S(1)}, u32[]{:S(2)}, u32[]{:S(2)}) collective-permute-start(f32[32,1,128,128]{3,0,2,1:T(8,128)S(1)} %get-tuple-element.5), channel_id=1, source_target_pairs={{0,1},{1,2},{2,3},{3,4},{4,5},{5,6},{6,7},{7,8},{8,9},{9,10},{10,1... | collective-permute-start | bytes 6291464 | tf_op jit(solution)/shard_map/ppermute | solution.py:19
  114.0 1.3 copy-start.4
  124.5 77.5 %copy-start.1 = (f32[32,2,128,128]{3,0,2,1:T(8,128)}, f32[32,2,128,128]{3,0,2,1:T(8,128)S(1)}, u32[]{:S(2)}) copy-start(f32[32,2,128,128]{3,0,2,1:T(8,128)S(1)} %fusion.27) | copy-start | bytes 12582916
  124.5 77.5 %collective-permute-start.4 = (f32[32,2,128,128]{3,0,2,1:T(8,128)S(1)}, f32[32,2,128,128]{3,0,2,1:T(8,128)S(1)}, u32[]{:S(2)}, u32[]{:S(2)}) collective-permute-start(f32[32,2,128,128]{3,0,2,1:T(8,128)S(1)} %fusion.27), channel_id=1, source_target_pairs={{32,0},{64,32},{96,64},{128,96},{160,128},{192,160},{224,192},{33,... | collective-permute-start | bytes 12582920 | tf_op jit(solution)/shard_map/ppermute | solution.py:28
  202.0 2.0 copy-start.3
  403.4 56.1 %copy-start = (f32[8,8,256,128]{3,2,1,0:T(8,128)}, f32[8,8,256,128]{3,2,1,0:T(8,128)S(1)}, u32[]{:S(2)}) copy-start(f32[8,8,256,128]{3,2,1,0:T(8,128)S(1)} %copy.14) | copy-start | bytes 25165828
  407.6 46.4 %collective-permute-start.5 = (f32[64,1,128,128]{3,2,1,0:T(8,128)}, f32[64,1,128,128]{3,2,1,0:T(8,128)}, u32[]{:S(2)}, u32[]{:S(2)}) collective-permute-start(f32[64,1,128,128]{3,2,1,0:T(8,128)} %get-tuple-element.2), channel_id=1, source_target_pairs={{1,0},{2,1},{3,2},{4,3},{5,4},{6,5},{7,6},{8,7},{9,8},{10,9},{11,1... | collective-permute-start | bytes 12582920 | tf_op jit(solution)/shard_map/ppermute | solution.py:20
  407.6 52.0 %collective-permute-start.6 = (f32[64,1,128,128]{3,2,1,0:T(8,128)}, f32[64,1,128,128]{3,2,1,0:T(8,128)}, u32[]{:S(2)}, u32[]{:S(2)}) collective-permute-start(f32[64,1,128,128]{3,2,1,0:T(8,128)} %get-tuple-element.3), channel_id=1, source_target_pairs={{0,1},{1,2},{2,3},{3,4},{4,5},{5,6},{6,7},{7,8},{8,9},{9,10},{10,1... | collective-permute-start | bytes 12582920 | tf_op jit(solution)/shard_map/ppermute | solution.py:19
